TPU v7x, 256 devices: a whole 4x4x8 slice. The times are simulated.
256 devices in a mesh: lat: 8 (over z_lo, core), lon: 8 (over z_hi, x), chan: 4 (over y).
Axes of the slice: x: 4, y: 4, z: 8 (z_hi: 2, z_lo: 4; z = z_hi * 4 + z_lo), core: 2. Of those that a mesh axis runs over, the one named last changes fastest.
Arguments:
- queries: bfloat16 [128, 64, 2560], P('lat', 'lon', 'chan'), may hold values from -8 to 8
- keys: bfloat16 [128, 64, 2560], P('lat', 'lon', 'chan'), may hold values from -8 to 8
- values: bfloat16 [128, 64, 2560], P('lat', 'lon', 'chan'), may hold values from -6 to 6
- attn_out: bfloat16 [128, 64, 2560], P('lat', 'lon', 'chan'), may hold values from -6 to 6
- grad_out: bfloat16 [128, 64, 5120], P('lat', 'lon', 'chan'), may hold values from -6 to 6
- w_out: bfloat16 [5120, 2560], P(('lat', 'lon'), 'chan'), may hold values from -0.078125 to 0.078125
- bias_table: float32 [20, 25, 13], P('chan'), may hold values from -5 to 5
- key_mask: int32 [128, 64], replicated, may hold values 0 or 1
Outputs:
- grad_queries: bfloat16 [128, 64, 2560], P('lat', 'lon', 'chan')
- grad_keys: bfloat16 [128, 64, 2560], P('lat', 'lon', 'chan')
- grad_values: bfloat16 [128, 64, 2560], P('lat', 'lon', 'chan')
- grad_wout: float32 [5120, 2560], P(('lat', 'lon'), 'chan')
- grad_table: float32 [20, 25, 13], P('chan')
All inputs are finite; a program needn't handle non-finite values.
Results may differ from a plain program's by a relative error of at most 0.007.
Values may be sent and summed in bfloat16 or wider, within the bound.
No kernel may reach another device: no remote copies, remote signals or barrier semaphores. Data moves between devices by JAX's collectives and lax.ppermute only.
A program may use at most 128 MiB of HBM per device.

v0:
```python
import jax
import jax.numpy as jnp
from jax import lax
from jax.sharding import PartitionSpec as P

HEAD_DIM = 128
WIN = 13


def extended_2(value, sides, width, wrap):
    for axis, dim in sides:
        count, length = (lax.axis_size(axis), value.shape[dim])
        up = [(i, (i + 1) % count) for i in range(count if wrap else count - 1)]
        down = [(j, i) for i, j in up]
        last = lax.slice_in_dim(value, length - width, length, axis=dim)
        leading = lax.slice_in_dim(value, 0, width, axis=dim)
        before = lax.ppermute(last, axis, up)
        after = lax.ppermute(leading, axis, down)
        value = jnp.concatenate([before, value, after], axis=dim)
    return value


def fold_lon(extended, core_width):
    full_width = extended.shape[2]
    reach_cells = (full_width - core_width) // 2
    rim_cells = jnp.concatenate(
        [extended[:, :, :reach_cells], extended[:, :, full_width - reach_cells :]], axis=2
    )
    received = extended_2(rim_cells.astype(jnp.bfloat16), (("lon", 2),), reach_cells, True).astype(
        rim_cells.dtype
    )
    middle = extended[:, :, reach_cells : full_width - reach_cells]
    front_add = jnp.pad(
        received[:, :, :reach_cells], ((0, 0), (0, 0), (0, core_width - reach_cells), (0, 0))
    )
    back_add = jnp.pad(
        received[:, :, 3 * reach_cells :], ((0, 0), (0, 0), (core_width - reach_cells, 0), (0, 0))
    )
    return middle + front_add + back_add


def fold_lat(extended, core_width):
    full_width = extended.shape[1]
    reach_cells = (full_width - core_width) // 2
    rim_cells = jnp.concatenate(
        [extended[:, :reach_cells], extended[:, full_width - reach_cells :]], axis=1
    )
    received = extended_2(rim_cells.astype(jnp.bfloat16), (("lat", 1),), reach_cells, False).astype(
        rim_cells.dtype
    )
    middle = extended[:, reach_cells : full_width - reach_cells]
    front_add = jnp.pad(
        received[:, :reach_cells], ((0, 0), (0, core_width - reach_cells), (0, 0), (0, 0))
    )
    back_add = jnp.pad(
        received[:, 3 * reach_cells :], ((0, 0), (core_width - reach_cells, 0), (0, 0), (0, 0))
    )
    return middle + front_add + back_add


def local(queries, keys, values, attn_out, grad_out, w_out, bias_table, key_mask):
    lat_rows, lon_cols, chan_width = queries.shape
    head_count = bias_table.shape[0]
    reach_cells = WIN // 2
    score_scale = HEAD_DIM ** (-0.5)
    tokens = lat_rows * lon_cols
    ext_rows = lat_rows + 2 * reach_cells
    ext_cols = lon_cols + 2 * reach_cells
    row_block = 4
    key_span = row_block + WIN - 1
    block_count = lat_rows // row_block
    block_rows = row_block * lon_cols
    block_keys = key_span * ext_cols
    offset_rows = 2 * WIN - 1
    low_pad = row_block - 1
    lat_total = lat_rows * lax.axis_size("lat")
    lon_total = lon_cols * lax.axis_size("lon")
    contract_lead = (((0,), (0,)), ((), ()))
    full_grad = lax.all_gather(grad_out, "chan", axis=2, tiled=True).reshape(tokens, -1)
    grad_cols = jnp.transpose(full_grad)
    slab_part = grad_cols
    grad_attn = lax.dot_general(
        slab_part,
        lax.all_gather(w_out, ("lat", "lon"), axis=0, tiled=True),
        contract_lead,
        preferred_element_type=jnp.float32,
    ).astype(jnp.bfloat16)
    kv_pair = jnp.stack([keys, values])
    extended = extended_2(kv_pair, (("lat", 1), ("lon", 2)), reach_cells, True)
    lat_first = lax.axis_index("lat") * lat_rows
    lon_first = lax.axis_index("lon") * lon_cols
    ext_col = lon_first - reach_cells + jnp.arange(ext_cols, dtype=jnp.int32)
    wrap_col = ext_col % lon_total
    mask_cols = jnp.take(key_mask, wrap_col, axis=1)
    mark_cols = wrap_col % 4 == 0
    rel_lon = (
        jnp.arange(ext_cols, dtype=jnp.int32)[None, :]
        - jnp.arange(lon_cols, dtype=jnp.int32)[:, None]
    )
    in_lon = (rel_lon >= 0) & (rel_lon < WIN)
    lon_pick = jnp.clip(rel_lon, 0, WIN - 1)
    lon_table = jnp.take(bias_table, lon_pick, axis=2).transpose(0, 2, 1, 3)
    table_pad = jnp.pad(lon_table, ((0, 0), (0, 0), (low_pad, low_pad), (0, 0)))
    query_heads = queries.reshape(lat_rows, lon_cols, head_count, HEAD_DIM)
    grad_heads = grad_attn.reshape(lat_rows, lon_cols, head_count, HEAD_DIM)

    def block_step(state_pair, block_index):
        grad_pair, table_acc = state_pair
        local_first = block_index * row_block
        top_row = lat_first + local_first
        key_first = jnp.clip(top_row - reach_cells, 0, lat_total - key_span)
        key_local = key_first - (lat_first - reach_cells)
        query_rows = top_row + jnp.arange(row_block, dtype=jnp.int32)
        window_first = jnp.clip(query_rows - reach_cells, 0, lat_total - WIN)
        key_glob = key_first + jnp.arange(key_span, dtype=jnp.int32)
        in_lat = (key_glob[None, :] >= window_first[:, None]) & (
            key_glob[None, :] < window_first[:, None] + WIN
        )
        mask_rows = lax.dynamic_slice_in_dim(mask_cols, key_first, key_span, 0)
        valid_keys = (mask_rows == 1) | (key_glob % 4 == 0)[:, None] & mark_cols[None, :]
        allowed = in_lat[:, None, :, None] & in_lon[None, :, None, :] & valid_keys[None, None, :, :]
        allowed = allowed.reshape(block_rows, block_keys)
        shifts = key_first - query_rows + (WIN - 1) + low_pad
        bias_parts = [
            lax.dynamic_slice_in_dim(table_pad, shifts[row_pos], key_span, 2)
            for row_pos in range(row_block)
        ]
        bias_rows = jnp.stack(bias_parts, axis=1).reshape(head_count, block_rows, block_keys)
        query_block = lax.dynamic_slice_in_dim(query_heads, local_first, row_block, 0).reshape(
            block_rows, head_count, HEAD_DIM
        )
        grad_block = lax.dynamic_slice_in_dim(grad_heads, local_first, row_block, 0).reshape(
            block_rows, head_count, HEAD_DIM
        )
        pair_block = lax.dynamic_slice_in_dim(extended, key_local, key_span, 1).reshape(
            2, block_keys, head_count, HEAD_DIM
        )
        key_block = pair_block[0]
        value_block = pair_block[1]
        scores = (
            score_scale
            * jnp.einsum("qhd,khd->hqk", query_block, key_block, preferred_element_type=jnp.float32)
            + bias_rows
        )
        scores = jnp.where(allowed[None], scores, -1e30)
        row_max = jnp.max(scores, axis=2, keepdims=True)
        weights_exp = jnp.exp(scores - row_max)
        prob_rows = weights_exp / jnp.sum(weights_exp, axis=2, keepdims=True)
        grad_prob = jnp.einsum(
            "qhd,khd->hqk", grad_block, value_block, preferred_element_type=jnp.float32
        )
        row_delta = jnp.sum(prob_rows * grad_prob, axis=2, keepdims=True)
        dscore = prob_rows * (grad_prob - row_delta)
        score_grid = dscore.reshape(head_count, row_block, lon_cols, key_span, ext_cols)
        score_grid = score_grid.transpose(0, 1, 3, 2, 4).reshape(
            head_count, row_block, key_span, lon_cols * ext_cols
        )
        for row_pos in range(row_block):
            prior_sum = lax.dynamic_slice_in_dim(table_acc, shifts[row_pos], key_span, 1)
            table_acc = lax.dynamic_update_slice_in_dim(
                table_acc, prior_sum + score_grid[:, row_pos], shifts[row_pos], 1
            )
        dscore_low = dscore.astype(jnp.bfloat16)
        prob_low = prob_rows.astype(jnp.bfloat16)
        grad_query = (
            score_scale
            * jnp.einsum("hqk,khd->qhd", dscore_low, key_block, preferred_element_type=jnp.float32)
        ).astype(jnp.bfloat16)
        key_part = score_scale * jnp.einsum(
            "hqk,qhd->khd", dscore_low, query_block, preferred_element_type=jnp.float32
        )
        value_part = jnp.einsum(
            "hqk,qhd->khd", prob_low, grad_block, preferred_element_type=jnp.float32
        )
        new_part = jnp.stack([key_part, value_part]).reshape(2, key_span, ext_cols, chan_width)
        prior_pair = lax.dynamic_slice_in_dim(grad_pair, key_local, key_span, 1)
        grad_pair = lax.dynamic_update_slice_in_dim(grad_pair, prior_pair + new_part, key_local, 1)
        return ((grad_pair, table_acc), grad_query)

    zero_pair = jnp.zeros((2, ext_rows, ext_cols, chan_width), jnp.float32)
    zero_table = jnp.zeros(
        (head_count, offset_rows + 2 * low_pad, lon_cols * ext_cols), jnp.float32
    )
    (grad_pair, table_acc), query_blocks = lax.scan(
        block_step, (zero_pair, zero_table), jnp.arange(block_count, dtype=jnp.int32)
    )
    grad_queries = query_blocks.reshape(lat_rows, lon_cols, chan_width)
    table_core = table_acc[:, low_pad : low_pad + offset_rows].reshape(
        head_count, offset_rows, lon_cols, ext_cols
    )
    col_take = (
        jnp.arange(lon_cols, dtype=jnp.int32)[:, None] + jnp.arange(WIN, dtype=jnp.int32)[None, :]
    )
    col_take = jnp.broadcast_to(
        col_take[None, None, :, :], (head_count, offset_rows, lon_cols, WIN)
    )
    table_local = jnp.sum(jnp.take_along_axis(table_core, col_take, axis=3), axis=2)
    grad_table = lax.psum(table_local, ("lat", "lon"))
    folded = fold_lat(fold_lon(grad_pair, lon_cols), lat_rows)
    grad_keys = folded[0].astype(jnp.bfloat16)
    grad_values = folded[1].astype(jnp.bfloat16)
    saved_out = attn_out.reshape(tokens, chan_width)
    slab_part = grad_cols
    grad_wout = lax.psum_scatter(
        jnp.dot(slab_part, saved_out, preferred_element_type=jnp.float32),
        ("lat", "lon"),
        scatter_dimension=0,
        tiled=True,
    )
    return (grad_queries, grad_keys, grad_values, grad_wout, grad_table)


def solution(mesh):
    return jax.shard_map(
        local,
        mesh=mesh,
        in_specs=(
            P("lat", "lon", "chan"),
            P("lat", "lon", "chan"),
            P("lat", "lon", "chan"),
            P("lat", "lon", "chan"),
            P("lat", "lon", "chan"),
            P(("lat", "lon"), "chan"),
            P("chan", None, None),
            P(),
        ),
        out_specs=(
            P("lat", "lon", "chan"),
            P("lat", "lon", "chan"),
            P("lat", "lon", "chan"),
            P(("lat", "lon"), "chan"),
            P("chan", None, None),
        ),
        check_vma=False,
    )
```

profile of v0, /device:TPU:240, one launch (start us, length us, event | category | flops | bytes accessed | tf_op | source)
XLA Modules:
  0.0 933.4 jit_solution(14924076082434811027)
XLA Ops:
  9.8 26.9 %all-gather.3.cloned.1.call-done = bf16[16,8,5120]{2,0,1:T(8,128)(2,1)} async-done(((bf16[16,8,1280]{2,0,1:T(8,128)(2,1)}), bf16[16,8,5120]{2,0,1:T(8,128)(2,1)}) %all-gather.3.cloned.1.call-update) | async-done | bytes 1310736 | tf_op jit(solution)/shard_map/all_gather | solution.py:79
  36.7 7.9 convolution_bitcast_fusion.1
  51.5 4.6 collective-permute-start.3
  59.1 11.4 %collective-permute-done.3 = bf16[2,28,6,640]{3,0,2,1:T(2,128)(2,1)S(1)} collective-permute-done((bf16[2,28,6,640]{3,0,2,1:T(2,128)(2,1)S(1)}, bf16[2,28,6,640]{3,0,2,1:T(2,128)(2,1)S(1)}, u32[]{:S(2)}, u32[]{:S(2)}) %collective-permute-start.3) | collective-permute-done | bytes 430112 | tf_op jit(solution)/shard_map/ppermute | solution.py:18
  70.6 10.3 %collective-permute-done.2 = bf16[2,28,6,640]{3,0,2,1:T(2,128)(2,1)S(1)} collective-permute-done((bf16[2,28,6,640]{3,0,2,1:T(2,128)(2,1)S(1)}, bf16[2,28,6,640]{3,0,2,1:T(2,128)(2,1)S(1)}, u32[]{:S(2)}, u32[]{:S(2)}) %collective-permute-start.2) | collective-permute-done | bytes 430112 | tf_op jit(solution)/shard_map/ppermute | solution.py:17
  80.9 2.1 pad_maximum_fusion.1
  83.0 156.4 %all-gather.5.cloned.1.call-done = bf16[5120,640]{1,0:T(8,128)(2,1)} async-done(((bf16[80,640]{1,0:T(8,128)(2,1)}), bf16[5120,640]{1,0:T(8,128)(2,1)}) %all-gather.5.cloned.1.call-update) | async-done | bytes 6553616 | tf_op jit(solution)/shard_map/all_gather | solution.py:84
  239.4 4.6 fusion.42
  244.0 1.9 broadcast_in_dim.94
  245.9 117.0 %while.18 = (s32[]{:T(128)}, f32[2,28,20,640]{3,2,1,0:T(8,128)}, f32[5,31,160]{2,1,0:T(8,128)S(1)}, bf16[4,32,5,128]{3,1,2,0:T(8,128)(2,1)}, s32[4]{0:T(128)S(1)...) while((s32[]{:T(128)}, f32[2,28,20,640]{3,2,1,0:T(8,128)}, ...), condition=%wide.region_4.5_spmd.clone, body=%wide.region_0.0_spmd.clone.sunk | while | flops 67648624 | bytes 32509632 | solution.py:184
  259.8 1.9 dynamic-slice_bitcast_fusion.5
  272.1 3.0 fusion.106
  301.4 3.0 fusion.106
  318.3 1.9 dynamic-slice_bitcast_fusion.5
  330.6 3.1 fusion.106
  347.5 1.9 dynamic-slice_bitcast_fusion.5
  359.8 3.1 fusion.106
  363.0 2.2 convert.16
  367.6 2.0 collective-permute-start.4
  371.3 155.3 %gather_fusion.2 = f32[13000]{0:T(1024)S(1)} fusion(f32[5,25,8,20]{3,2,1,0:T(8,128)S(1)} %reshape.333, s32[13000]{0:T(1024)S(1)} %reshape.350), kind=kCustom, calls=%fused_computation.2 | custom fusion | bytes 312000 | tf_op jit(solution)/shard_map/jit(take_along_axis)/gather | solution.py:197
  529.9 2.3 fusion.59
  532.3 2.1 collective-permute-start.6
  534.3 4.4 collective-permute-start.7
  539.0 386.1 %psum.7 = f32[5,25,13]{2,1,0:T(8,128)S(1)} all-reduce(f32[5,25,13]{2,1,0:T(8,128)S(1)} %select_reduce_fusion), channel_id=1, replica_groups=mesh['lat'=8,'lon'=8,'chan'=4] {'lat','lon'}, use_global_device_ids=true, to_apply=%region_7.8 | all-reduce | flops 1625 | bytes 13000 | tf_op jit(solution)/shard_map/psum | solution.py:198
  (305 shorter events, 87.1 us)
Async XLA Ops:
  7.2 29.5 %copy-start = (bf16[16,8,640]{2,1,0:T(8,128)(2,1)S(1)}, bf16[16,8,640]{2,1,0:T(8,128)(2,1)}, u32[]{:S(2)}) copy-start(bf16[16,8,640]{2,1,0:T(8,128)(2,1)} %param.13) | copy-start | bytes 491524
  7.2 29.5 %all-gather.3.cloned.1.call-start = ((), (), s32[]{:S(2)}) async-start(), calls=%async_computation.1 | async-start | bytes 1638400 | tf_op jit(solution)/shard_map/all_gather | solution.py:79
  9.0 230.4 %all-gather.5.cloned.1.call-start = ((), (), s32[]{:S(2)}) async-start(), calls=%async_computation.2 | async-start | bytes 6656000 | tf_op jit(solution)/shard_map/all_gather | solution.py:84
  9.8 917.1 %reduce-scatter.2.cloned.1.call-start = ((), (), s32[]{:S(2)}) async-start(), calls=%async_computation.3 | async-start | bytes 13312000 | tf_op jit(solution)/shard_map/reduce_scatter | solution.py:204
  45.7 4.4 collective-permute-start
  45.8 4.8 collective-permute-start.1
  50.6 5.5 copy-start.1
  51.5 19.0 %collective-permute-start.3 = (bf16[2,28,6,640]{3,0,2,1:T(2,128)(2,1)S(1)}, bf16[2,28,6,640]{3,0,2,1:T(2,128)(2,1)S(1)}, u32[]{:S(2)}, u32[]{:S(2)}) collective-permute-start(bf16[2,28,6,640]{3,0,2,1:T(2,128)(2,1)S(1)} %copy.59), channel_id=1, source_target_pairs={{4,0},{8,4},{12,8},{16,12},{20,16},{24,20},{28,24},{0,28},{5,1},{9... | collective-permute-start | bytes 1290248 | tf_op jit(solution)/shard_map/ppermute | solution.py:18
  56.1 24.7 %collective-permute-start.2 = (bf16[2,28,6,640]{3,0,2,1:T(2,128)(2,1)S(1)}, bf16[2,28,6,640]{3,0,2,1:T(2,128)(2,1)S(1)}, u32[]{:S(2)}, u32[]{:S(2)}) collective-permute-start(bf16[2,28,6,640]{3,0,2,1:T(2,128)(2,1)S(1)} %copy.58), channel_id=1, source_target_pairs={{0,4},{4,8},{8,12},{12,16},{16,20},{20,24},{24,28},{28,0},{1,5},{5... | collective-permute-start | bytes 1290248 | tf_op jit(solution)/shard_map/ppermute | solution.py:17
  80.9 158.5 %copy-start.11 = (bf16[16,8,5120]{2,0,1:T(8,128)(2,1)S(1)}, bf16[16,8,5120]{2,0,1:T(8,128)(2,1)}, u32[]{:S(2)}) copy-start(bf16[16,8,5120]{2,0,1:T(8,128)(2,1)} %all-gather.3.cloned.1.call-done) | copy-start | bytes 3932164
  245.9 13.4 %copy-start.12 = (bf16[16,8,5,128]{3,1,2,0:T(8,128)(2,1)}, bf16[16,8,5,128]{3,1,2,0:T(8,128)(2,1)S(1)}, u32[]{:S(2)}) copy-start(bf16[16,8,5,128]{3,1,2,0:T(8,128)(2,1)S(1)} %get-tuple-element.541) | copy-start | bytes 491524 | tf_op jit(solution)/shard_map/while
  275.2 13.4 %copy-start.12 = (bf16[16,8,5,128]{3,1,2,0:T(8,128)(2,1)}, bf16[16,8,5,128]{3,1,2,0:T(8,128)(2,1)S(1)}, u32[]{:S(2)}) copy-start(bf16[16,8,5,128]{3,1,2,0:T(8,128)(2,1)S(1)} %get-tuple-element.541) | copy-start | bytes 491524 | tf_op jit(solution)/shard_map/while
  304.4 13.4 %copy-start.12 = (bf16[16,8,5,128]{3,1,2,0:T(8,128)(2,1)}, bf16[16,8,5,128]{3,1,2,0:T(8,128)(2,1)S(1)}, u32[]{:S(2)}) copy-start(bf16[16,8,5,128]{3,1,2,0:T(8,128)(2,1)S(1)} %get-tuple-element.541) | copy-start | bytes 491524 | tf_op jit(solution)/shard_map/while
  333.6 13.4 %copy-start.12 = (bf16[16,8,5,128]{3,1,2,0:T(8,128)(2,1)}, bf16[16,8,5,128]{3,1,2,0:T(8,128)(2,1)S(1)}, u32[]{:S(2)}) copy-start(bf16[16,8,5,128]{3,1,2,0:T(8,128)(2,1)S(1)} %get-tuple-element.541) | copy-start | bytes 491524 | tf_op jit(solution)/shard_map/while
  365.3 4.3 copy-start.4
  365.3 4.7 copy-start.14
  367.6 159.4 %collective-permute-start.5 = (bf16[2,28,6,640]{3,0,2,1:T(2,128)(2,1)}, bf16[2,28,6,640]{3,0,2,1:T(2,128)(2,1)}, u32[]{:S(2)}, u32[]{:S(2)}) collective-permute-start(bf16[2,28,6,640]{3,0,2,1:T(2,128)(2,1)} %copy.71), channel_id=1, source_target_pairs={{4,0},{8,4},{12,8},{16,12},{20,16},{24,20},{28,24},{0,28},{5,1},{9... | collective-permute-start | bytes 1290248 | tf_op jit(solution)/shard_map/ppermute | solution.py:18
  367.6 160.5 %collective-permute-start.4 = (bf16[2,28,6,640]{3,0,2,1:T(2,128)(2,1)}, bf16[2,28,6,640]{3,0,2,1:T(2,128)(2,1)}, u32[]{:S(2)}, u32[]{:S(2)}) collective-permute-start(bf16[2,28,6,640]{3,0,2,1:T(2,128)(2,1)} %copy.70), channel_id=1, source_target_pairs={{0,4},{4,8},{8,12},{12,16},{16,20},{20,24},{24,28},{28,0},{1,5},{5... | collective-permute-start | bytes 1290248 | tf_op jit(solution)/shard_map/ppermute | solution.py:17
  529.9 8.9 copy-start.16
  529.9 8.9 copy-start.18
  529.9 8.9 copy-start.20
  532.2 393.8 %copy-start.22 = (pred[16]{0:T(512)(128)(4,1)S(1)}, pred[16]{0:T(512)(128)(4,1)}, u32[]{:S(2)}) copy-start(pred[16]{0:T(512)(128)(4,1)} %constant.227.clone.1) | copy-start | bytes 52
  532.3 393.6 %collective-permute-start.6 = (bf16[2,6,8,640]{3,2,1,0:T(8,128)(2,1)S(1)}, bf16[2,6,8,640]{3,2,1,0:T(8,128)(2,1)S(1)}, u32[]{:S(2)}, u32[]{:S(2)}) collective-permute-start(bf16[2,6,8,640]{3,2,1,0:T(8,128)(2,1)S(1)} %get-tuple-element.361), channel_id=1, source_target_pairs={{0,32},{32,64},{64,96},{96,128},{128,160},{160,192},{192,224},{1,3... | collective-permute-start | bytes 368648 | tf_op jit(solution)/shard_map/ppermute | solution.py:17
  534.3 391.5 %collective-permute-start.7 = (bf16[2,6,8,640]{3,2,1,0:T(8,128)(2,1)S(1)}, bf16[2,6,8,640]{3,2,1,0:T(8,128)(2,1)S(1)}, u32[]{:S(2)}, u32[]{:S(2)}) collective-permute-start(bf16[2,6,8,640]{3,2,1,0:T(8,128)(2,1)S(1)} %get-tuple-element.362), channel_id=1, source_target_pairs={{32,0},{64,32},{96,64},{128,96},{160,128},{192,160},{224,192},{33,... | collective-permute-start | bytes 368648 | tf_op jit(solution)/shard_map/ppermute | solution.py:18
  (22 other events, 43.6 us)
Sparse Core Ops, SparseCore 0:
  9.8 26.8 all-gather.2
  38.5 200.8 all-gather.4
  242.6 461.3 reduce-scatter.1
where the time goes:
time: 935 us; the launch traced here: 933 us
  blocking collectives  386 us (41%)
  local copies, waits for them, and re-layouts  227 us (24%)
  waiting for transfers between devices  207 us (22%)
  loops' own time  33.7 us (4%)
  other arithmetic  28.7 us (3%)
  matrix products  21.7 us (2%)
  starting transfers between devices  15.1 us (2%)
  between operations  14.2 us (2%)
    psum x1, blocking collectives, local(): grad_table = lax.psum(table_local, ('lat', 'lon'))  386 us
    all_gather x1, waiting for transfers between devices, local(): lax.all_gather(w_out, ('lat', 'lon'), axis=0, tiled=True)  156 us
    gather x3, local copies, waits for them, and re-layouts, local(): jnp.take_along_axis(table_core, col_take, axis=3)  156 us
    another operation x1, loops' own time, local(): lax.scan(block_step, (zero_pair, zero_table), jnp.arange(block_count, dty...  33.7 us
    all_gather x1, waiting for transfers between devices, local(): lax.all_gather(grad_out, 'chan', axis=2, tiled=True).reshape(tokens, -1)  26.9 us
  transfers between devices with their start and end apart: 11, of which 6 were waited for; matrix products, arithmetic and copies ran while one was open for 29% of the time, Pallas kernels for 0%

commit v1 on v0

--- a/solution.py
+++ b/solution.py
@@ -195,7 +195,7 @@
         col_take[None, None, :, :], (head_count, offset_rows, lon_cols, WIN)
     )
     table_local = jnp.sum(jnp.take_along_axis(table_core, col_take, axis=3), axis=2)
-    grad_table = lax.psum(table_local, ("lat", "lon"))
+    grad_table = jnp.sum(lax.all_gather(table_local, ("lat", "lon")), axis=0)
     folded = fold_lat(fold_lon(grad_pair, lon_cols), lat_rows)
     grad_keys = folded[0].astype(jnp.bfloat16)
     grad_values = folded[1].astype(jnp.bfloat16)

time: 935 us -> 802 us (0.86)
  blocking collectives: 386 us -> 248 us
    psum x1 -> x0, blocking collectives: 386 us -> none  [local(): grad_table = lax.psum(table_local, ('lat', 'lon'))]
    all_gather x0 -> x1, blocking collectives: none -> 248 us  [local(): grad_table = jnp.sum(lax.all_gather(table_local, ('lat', 'lon')), axis=0)]
  transfers between devices with their start and end apart: 11 -> 11, of which waited for: 6 -> 5; matrix products, arithmetic and copies ran while one was open for 29% -> 34% of each run, Pallas kernels for 0% -> 0%
where the time goes in v1:
time: 802 us; the launch traced here: 793 us
  blocking collectives  248 us (31%)
  local copies, waits for them, and re-layouts  226 us (28%)
  waiting for transfers between devices  209 us (26%)
  loops' own time  34.3 us (4%)
  other arithmetic  27.9 us (3%)
  matrix products  20 us (2%)
  starting transfers between devices  14.4 us (2%)
  between operations  14.1 us (2%)
    all_gather x1, blocking collectives, local(): grad_table = jnp.sum(lax.all_gather(table_local, ('lat', 'lon')), axis=0)  248 us
    all_gather x1, waiting for transfers between devices, local(): lax.all_gather(w_out, ('lat', 'lon'), axis=0, tiled=True)  156 us
    gather x3, local copies, waits for them, and re-layouts, local(): jnp.take_along_axis(table_core, col_take, axis=3)  156 us
    another operation x1, loops' own time, local(): lax.scan(block_step, (zero_pair, zero_table), jnp.arange(block_count, dty...  34.3 us
    all_gather x1, waiting for transfers between devices, local(): lax.all_gather(grad_out, 'chan', axis=2, tiled=True).reshape(tokens, -1)  26.9 us
  transfers between devices with their start and end apart: 11, of which 5 were waited for; matrix products, arithmetic and copies ran while one was open for 34% of the time, Pallas kernels for 0%

profile of v1, /device:TPU:240, one launch (start us, length us, event | category | flops | bytes accessed | tf_op | source)
XLA Modules:
  0.0 793.0 jit_solution(16007302181598063708)
XLA Ops:
  9.8 26.9 %all-gather.4.cloned.1.call-done = bf16[16,8,5120]{2,0,1:T(8,128)(2,1)} async-done(((bf16[16,8,1280]{2,0,1:T(8,128)(2,1)}), bf16[16,8,5120]{2,0,1:T(8,128)(2,1)}) %all-gather.4.cloned.1.call-update) | async-done | bytes 1310736 | tf_op jit(solution)/shard_map/all_gather | solution.py:79
  36.7 7.9 %convolution_bitcast_fusion.1 = f32[5120,640]{1,0:T(8,128)} fusion(bf16[16,8,5120]{2,0,1:T(8,128)(2,1)} %all-gather.4.cloned.1.call-done, bf16[16,8,640]{2,1,0:T(8,128)(2,1)S(1)} %copy-done), kind=kOutput, calls=%fused_computation.77 | convolution fusion | flops 838860800 | bytes 14581760 | tf_op jit(solution)/shard_map/dot_general | solution.py:205
  51.5 4.8 collective-permute-start.3
  57.5 12.8 %collective-permute-done.3 = bf16[2,28,6,640]{3,0,2,1:T(2,128)(2,1)S(1)} collective-permute-done((bf16[2,28,6,640]{3,0,2,1:T(2,128)(2,1)S(1)}, bf16[2,28,6,640]{3,0,2,1:T(2,128)(2,1)S(1)}, u32[]{:S(2)}, u32[]{:S(2)}) %collective-permute-start.3) | collective-permute-done | bytes 430112 | tf_op jit(solution)/shard_map/ppermute | solution.py:18
  70.4 11.9 %collective-permute-done.2 = bf16[2,28,6,640]{3,0,2,1:T(2,128)(2,1)S(1)} collective-permute-done((bf16[2,28,6,640]{3,0,2,1:T(2,128)(2,1)S(1)}, bf16[2,28,6,640]{3,0,2,1:T(2,128)(2,1)S(1)}, u32[]{:S(2)}, u32[]{:S(2)}) %collective-permute-start.2) | collective-permute-done | bytes 430112 | tf_op jit(solution)/shard_map/ppermute | solution.py:17
  82.4 2.1 pad_maximum_fusion.1
  84.4 156.1 %all-gather.6.cloned.1.call-done = bf16[5120,640]{1,0:T(8,128)(2,1)} async-done(((bf16[80,640]{1,0:T(8,128)(2,1)}), bf16[5120,640]{1,0:T(8,128)(2,1)}) %all-gather.6.cloned.1.call-update) | async-done | bytes 6553616 | tf_op jit(solution)/shard_map/all_gather | solution.py:84
  240.5 5.2 fusion.42
  245.7 1.9 broadcast_in_dim.94
  247.7 112.3 %while.18 = (s32[]{:T(128)}, f32[2,28,20,640]{3,2,1,0:T(8,128)}, f32[5,31,160]{2,1,0:T(8,128)S(1)}, bf16[4,32,5,128]{3,1,2,0:T(8,128)(2,1)S(1)}, s32[4]{0:T(128)...) while((s32[]{:T(128)}, f32[2,28,20,640]{3,2,1,0:T(8,128)}, ...), condition=%wide.region_4.5_spmd.clone, body=%wide.region_0.0_spmd.clone.sunk | while | flops 67648624 | bytes 32878328 | solution.py:184
  272.7 3.1 fusion.106
  289.0 1.9 dynamic-slice_bitcast_fusion.5
  300.8 3.1 fusion.106
  317.1 1.9 dynamic-slice_bitcast_fusion.5
  328.8 3.1 fusion.106
  345.1 1.9 dynamic-slice_bitcast_fusion.5
  356.9 3.1 fusion.106
  360.0 2.2 convert.16
  364.6 2.0 collective-permute-start.4
  368.3 155.1 %gather_fusion.2 = f32[13000]{0:T(1024)S(1)} fusion(f32[5,25,8,20]{3,2,1,0:T(8,128)S(1)} %reshape.333, s32[13000]{0:T(1024)S(1)} %reshape.350), kind=kCustom, calls=%fused_computation.2 | custom fusion | bytes 312000 | tf_op jit(solution)/shard_map/jit(take_along_axis)/gather | solution.py:197
  526.9 3.3 fusion.59
  530.3 1.9 collective-permute-start.6
  532.2 3.7 collective-permute-start.7
  535.9 247.6 %all-gather = f32[320,25,13]{1,2,0:T(8,128)S(1)} all-gather(f32[5,25,13]{1,2,0:T(8,128)S(1)} %copy.97), channel_id=2, replica_groups=mesh['lat'=8,'lon'=8,'chan'=4] {'lat','lon'}, dimensions={0}, use_global_device_ids=true | all-gather | bytes 422500 | tf_op jit(solution)/shard_map/all_gather | solution.py:198
  (312 shorter events, 81.2 us)
Async XLA Ops:
  7.2 29.5 %copy-start = (bf16[16,8,640]{2,1,0:T(8,128)(2,1)S(1)}, bf16[16,8,640]{2,1,0:T(8,128)(2,1)}, u32[]{:S(2)}) copy-start(bf16[16,8,640]{2,1,0:T(8,128)(2,1)} %param.13) | copy-start | bytes 491524
  7.2 29.5 %all-gather.4.cloned.1.call-start = ((), (), s32[]{:S(2)}) async-start(), calls=%async_computation.1 | async-start | bytes 1638400 | tf_op jit(solution)/shard_map/all_gather | solution.py:79
  9.0 231.5 %all-gather.6.cloned.1.call-start = ((), (), s32[]{:S(2)}) async-start(), calls=%async_computation.2 | async-start | bytes 6656000 | tf_op jit(solution)/shard_map/all_gather | solution.py:84
  9.8 776.7 %reduce-scatter.2.cloned.1.call-start = ((), (), s32[]{:S(2)}) async-start(), calls=%async_computation.3 | async-start | bytes 13312000 | tf_op jit(solution)/shard_map/reduce_scatter | solution.py:204
  44.7 3.7 copy-start.2
  45.7 4.6 collective-permute-start
  45.8 4.8 collective-permute-start.1
  51.5 18.8 %collective-permute-start.3 = (bf16[2,28,6,640]{3,0,2,1:T(2,128)(2,1)S(1)}, bf16[2,28,6,640]{3,0,2,1:T(2,128)(2,1)S(1)}, u32[]{:S(2)}, u32[]{:S(2)}) collective-permute-start(bf16[2,28,6,640]{3,0,2,1:T(2,128)(2,1)S(1)} %copy.81), channel_id=1, source_target_pairs={{4,0},{8,4},{12,8},{16,12},{20,16},{24,20},{28,24},{0,28},{5,1},{9... | collective-permute-start | bytes 1290248 | tf_op jit(solution)/shard_map/ppermute | solution.py:18
  56.4 25.9 %collective-permute-start.2 = (bf16[2,28,6,640]{3,0,2,1:T(2,128)(2,1)S(1)}, bf16[2,28,6,640]{3,0,2,1:T(2,128)(2,1)S(1)}, u32[]{:S(2)}, u32[]{:S(2)}) collective-permute-start(bf16[2,28,6,640]{3,0,2,1:T(2,128)(2,1)S(1)} %copy.80), channel_id=1, source_target_pairs={{0,4},{4,8},{8,12},{12,16},{16,20},{20,24},{24,28},{28,0},{1,5},{5... | collective-permute-start | bytes 1290248 | tf_op jit(solution)/shard_map/ppermute | solution.py:17
  82.3 158.2 %copy-start.13 = (bf16[16,8,5120]{2,0,1:T(8,128)(2,1)S(1)}, bf16[16,8,5120]{2,0,1:T(8,128)(2,1)}, u32[]{:S(2)}) copy-start(bf16[16,8,5120]{2,0,1:T(8,128)(2,1)} %all-gather.4.cloned.1.call-done) | copy-start | bytes 3932164
  247.7 12.3 %copy-start.14 = (s32[128,20]{1,0:T(8,128)}, s32[128,20]{1,0:T(8,128)S(1)}, u32[]{:S(2)}) copy-start(s32[128,20]{1,0:T(8,128)S(1)} %get-tuple-element.541) | copy-start | bytes 30724 | tf_op jit(solution)/shard_map/while
  272.7 3.1 copy-start.15
  272.7 3.1 copy-start.17
  275.8 12.3 %copy-start.14 = (s32[128,20]{1,0:T(8,128)}, s32[128,20]{1,0:T(8,128)S(1)}, u32[]{:S(2)}) copy-start(s32[128,20]{1,0:T(8,128)S(1)} %get-tuple-element.541) | copy-start | bytes 30724 | tf_op jit(solution)/shard_map/while
  303.8 12.3 %copy-start.14 = (s32[128,20]{1,0:T(8,128)}, s32[128,20]{1,0:T(8,128)S(1)}, u32[]{:S(2)}) copy-start(s32[128,20]{1,0:T(8,128)S(1)} %get-tuple-element.541) | copy-start | bytes 30724 | tf_op jit(solution)/shard_map/while
  331.9 12.3 %copy-start.14 = (s32[128,20]{1,0:T(8,128)}, s32[128,20]{1,0:T(8,128)S(1)}, u32[]{:S(2)}) copy-start(s32[128,20]{1,0:T(8,128)S(1)} %get-tuple-element.541) | copy-start | bytes 30724 | tf_op jit(solution)/shard_map/while
  356.9 3.1 copy-start.15
  356.9 3.1 copy-start.17
  362.4 4.3 copy-start.5
  362.4 4.3 copy-start.7
  364.6 159.4 %collective-permute-start.5 = (bf16[2,28,6,640]{3,0,2,1:T(2,128)(2,1)}, bf16[2,28,6,640]{3,0,2,1:T(2,128)(2,1)}, u32[]{:S(2)}, u32[]{:S(2)}) collective-permute-start(bf16[2,28,6,640]{3,0,2,1:T(2,128)(2,1)} %copy.93), channel_id=1, source_target_pairs={{4,0},{8,4},{12,8},{16,12},{20,16},{24,20},{28,24},{0,28},{5,1},{9... | collective-permute-start | bytes 1290248 | tf_op jit(solution)/shard_map/ppermute | solution.py:18
  364.6 160.5 %collective-permute-start.4 = (bf16[2,28,6,640]{3,0,2,1:T(2,128)(2,1)}, bf16[2,28,6,640]{3,0,2,1:T(2,128)(2,1)}, u32[]{:S(2)}, u32[]{:S(2)}) collective-permute-start(bf16[2,28,6,640]{3,0,2,1:T(2,128)(2,1)} %copy.92), channel_id=1, source_target_pairs={{0,4},{4,8},{8,12},{12,16},{16,20},{20,24},{24,28},{28,0},{1,5},{5... | collective-permute-start | bytes 1290248 | tf_op jit(solution)/shard_map/ppermute | solution.py:17
  530.3 254.1 %collective-permute-start.6 = (bf16[2,6,8,640]{3,2,1,0:T(8,128)(2,1)S(1)}, bf16[2,6,8,640]{3,2,1,0:T(8,128)(2,1)S(1)}, u32[]{:S(2)}, u32[]{:S(2)}) collective-permute-start(bf16[2,6,8,640]{3,2,1,0:T(8,128)(2,1)S(1)} %get-tuple-element.364), channel_id=1, source_target_pairs={{0,32},{32,64},{64,96},{96,128},{128,160},{160,192},{192,224},{1,3... | collective-permute-start | bytes 368648 | tf_op jit(solution)/shard_map/ppermute | solution.py:17
  532.2 252.1 %collective-permute-start.7 = (bf16[2,6,8,640]{3,2,1,0:T(8,128)(2,1)S(1)}, bf16[2,6,8,640]{3,2,1,0:T(8,128)(2,1)S(1)}, u32[]{:S(2)}, u32[]{:S(2)}) collective-permute-start(bf16[2,6,8,640]{3,2,1,0:T(8,128)(2,1)S(1)} %get-tuple-element.365), channel_id=1, source_target_pairs={{32,0},{64,32},{96,64},{128,96},{160,128},{192,160},{224,192},{33,... | collective-permute-start | bytes 368648 | tf_op jit(solution)/shard_map/ppermute | solution.py:18
  (25 other events, 48.5 us)
Sparse Core Ops, SparseCore 0:
  9.8 26.8 all-gather.3
  38.5 201.9 all-gather.5
  243.6 492.6 reduce-scatter.1
